TPU v7x, 32 devices: a whole 2x2x4 slice. The times are simulated.
32 devices in a mesh: sub: 8 (over z, y), col: 4 (over x, core).
Axes of the slice: x: 2, y: 2, z: 4, core: 2. Of those that a mesh axis runs over, the one named last changes fastest.
Arguments:
- rhs: bfloat16 [32, 1024, 128], P(('sub', 'col')), may hold values from -64 to 64
- schur: bfloat16 [32, 1024, 1024], P(('sub', 'col')), may hold values from -1 to 3
- local_inverse: bfloat16 [32, 1024, 1024], P(('sub', 'col')), may hold values from -1 to 2
- basis: bfloat16 [32, 8, 1024], P(('sub', 'col')), may hold values from -0.75 to 0.75
- coarse_inverse: bfloat16 [256, 256], P('sub', 'col'), may hold values from -1 to 2
- primal_index: int32 [32, 8], P(('sub', 'col')), may hold values from 0 to 255, as said below
- neighbour_dof: int32 [32, 1024], P(('sub', 'col')), may hold values from 0 to 1023, as said below
Outputs:
- solution: bfloat16 [32, 1024, 128], P(('sub', 'col'))
Inputs may be any that keep to these rules, and one draw needn't show every extreme that they name: `neighbour_dof`: each subdomain's unknowns in one shared block name places in the neighbour's facing block (for [0, 256) the neighbour's [256, 512), and so on), and the neighbour's entry names the place back. `primal_index`: every coarse unknown is named exactly once over all subdomains.
All inputs are finite; a program needn't handle non-finite values.
Results may differ from a plain program's by a relative error of at most 0.004.
The roundings to bfloat16 on the way count: a program that leaves them out, or rounds other values in their place, can miss the bound.
Values may be sent and summed in bfloat16 or wider, within the bound.
A program may use at most 64 MiB of HBM per device.

v0:
```python
import jax
import jax.numpy as jnp
from jax import lax
from jax.sharding import PartitionSpec as P


def from_behind(value, axis, steps):
    count = lax.axis_size(axis)
    pairs = [(source, (source + steps) % count) for source in range(count)]
    return lax.ppermute(value, axis, pairs)


def on_device(rhs, schur, local_inverse, basis, coarse_inverse, primal_index, neighbour_dof):
    link_table = neighbour_dof[0]
    face_size = link_table.shape[0] // 4
    cases = rhs.shape[2]
    offsets = (face_size, 0, 3 * face_size, 2 * face_size)
    places = []
    for number in range(4):
        places.append(link_table[number * face_size : (number + 1) * face_size] - offsets[number])
    schur_own = schur[0]
    inverse_own = local_inverse[0]
    basis_own = basis[0]
    index_own = primal_index[0]
    column_width = coarse_inverse.shape[1]
    column_base = lax.axis_index("col") * column_width

    def combine(field, incoming):
        collected = [
            jnp.take(incoming[number].astype(jnp.float32), places[number], axis=0)
            for number in range(4)
        ]
        return field + jnp.concatenate(collected, axis=0)

    def assemble(field):
        from_below = from_behind(field[face_size : 2 * face_size], "sub", 1)
        from_above = from_behind(field[:face_size], "sub", -1)
        from_left = from_behind(field[3 * face_size :].astype(jnp.bfloat16), "col", 1).astype(
            jnp.float32
        )
        from_right = from_behind(field[2 * face_size : 3 * face_size], "col", -1)
        return combine(field, (from_below, from_above, from_left, from_right))

    def inner(left_field, right_field):
        return lax.psum(0.5 * jnp.sum(left_field * right_field, axis=0), ("sub", "col"))

    residual = assemble(rhs[0].astype(jnp.float32))
    weighted = (residual * 0.5).astype(jnp.bfloat16)
    local_part = jnp.dot(inverse_own, weighted, preferred_element_type=jnp.float32)
    coarse_load = jnp.dot(basis_own, weighted, preferred_element_type=jnp.float32).astype(
        jnp.bfloat16
    )
    start_block = jnp.zeros((column_width, cases), jnp.bfloat16)
    values = lax.all_gather(coarse_load, ("sub", "col"), axis=0, tiled=True)
    indices = lax.all_gather(index_own, ("sub", "col"), axis=0, tiled=True)
    spots = indices - column_base
    spots = jnp.where((spots >= 0) & (spots < column_width), spots, column_width)
    column_part = start_block.at[spots].set(values, mode="drop")
    partial_rows = jnp.dot(coarse_inverse, column_part, preferred_element_type=jnp.float32)
    start_taken = jnp.zeros((index_own.shape[0], cases), jnp.bfloat16)
    block_rows = lax.psum(partial_rows, "col").astype(jnp.bfloat16)
    piece = lax.all_gather(block_rows, "sub", axis=0, tiled=True)
    spots = index_own
    count = piece.shape[0]
    valid = (spots >= 0) & (spots < count)
    rows = jnp.take(piece, jnp.clip(spots, 0, count - 1), axis=0)
    taken = jnp.where(valid[:, None], rows, start_taken)
    correction = lax.dot_general(
        basis_own, taken, (((0,), (0,)), ((), ())), preferred_element_type=jnp.float32
    )
    first = assemble((local_part + correction) * 0.5)
    rz_first = inner(residual, first)
    image = assemble(
        jnp.dot(schur_own, first.astype(jnp.bfloat16), preferred_element_type=jnp.float32)
    )
    alpha = rz_first / inner(first, image)
    return (alpha * first).astype(jnp.bfloat16)[None]


def solution(mesh):
    return jax.shard_map(
        on_device,
        mesh=mesh,
        in_specs=(
            P(("sub", "col"), None, None),
            P(("sub", "col"), None, None),
            P(("sub", "col"), None, None),
            P(("sub", "col"), None, None),
            P("sub", "col"),
            P(("sub", "col"), None),
            P(("sub", "col"), None),
        ),
        out_specs=P(("sub", "col"), None, None),
        check_vma=False,
    )
```

profile of v0, /device:TPU:0, one launch (start us, length us, event | category | flops | bytes accessed | tf_op | source)
XLA Modules:
  0.0 225.9 jit_solution(8289083633915082191)
XLA Ops:
  0.0 1.2 copy.8
  1.3 3.1 %collective-permute-start = (f32[256,128]{0,1:T(8,128)S(1)}, f32[256,128]{0,1:T(8,128)S(1)}, u32[]{:S(2)}, u32[]{:S(2)}) collective-permute-start(f32[256,128]{0,1:T(8,128)S(1)} %get-tuple-element.16), channel_id=1, source_target_pairs={{0,4},{4,8},{8,12},{12,16},{16,20},{20,24},{24,28},{28,0},{1,5},{5... | collective-permute-start | bytes 393224 | tf_op jit(solution)/shard_map/ppermute | solution.py:10
  4.4 3.1 %collective-permute-start.1 = (f32[256,128]{0,1:T(8,128)S(1)}, f32[256,128]{0,1:T(8,128)S(1)}, u32[]{:S(2)}, u32[]{:S(2)}) collective-permute-start(f32[256,128]{0,1:T(8,128)S(1)} %get-tuple-element.17), channel_id=1, source_target_pairs={{0,28},{4,0},{8,4},{12,8},{16,12},{20,16},{24,20},{28,24},{1,29},{... | collective-permute-start | bytes 393224 | tf_op jit(solution)/shard_map/ppermute | solution.py:10
  12.6 37.7 %all-reduce = s32[256]{0:T(256)S(1)} all-reduce(s32[256]{0:T(256)S(1)} %bitcast_dynamic-update-slice_fusion), channel_id=2, replica_groups=mesh['sub'=8,'col'=4] {'sub','col'}, use_global_device_ids=true, to_apply=%add | all-reduce | flops 256 | bytes 2048
  52.9 1.2 broadcast_select_fusion.9
  57.4 41.2 %all_gather.10 = bf16[256,128]{1,0:T(8,128)(2,1)S(1)} all-gather(bf16[8,128]{1,0:T(8,128)(2,1)S(1)} %fusion.9), channel_id=1, replica_groups=mesh['sub'=8,'col'=4] {'sub','col'}, dimensions={0}, use_global_device_ids=true | all-gather | bytes 67584 | tf_op jit(solution)/shard_map/all_gather | solution.py:54
  98.6 1.3 scatter_custom_fusion
  100.0 10.3 %psum.21 = bf16[32,128]{1,0:T(8,128)(2,1)S(1)} all-reduce(f32[32,128]{1,0:T(8,128)S(1)} %convolution_bitcast_fusion), channel_id=1, replica_groups=mesh['sub'=8,'col'=4] {'col'}, use_global_device_ids=true, to_apply=%region_1.3 | all-reduce | flops 4096 | bytes 24576 | tf_op jit(solution)/shard_map/psum | solution.py:61
  110.4 30.5 %all_gather.11 = bf16[256,128]{1,0:T(8,128)(2,1)S(1)} all-gather(bf16[32,128]{1,0:T(8,128)(2,1)S(1)} %psum.21), channel_id=1, replica_groups=mesh['sub'=8,'col'=4] {'sub'}, dimensions={0}, use_global_device_ids=true | all-gather | bytes 73728 | tf_op jit(solution)/shard_map/all_gather | solution.py:62
  140.9 1.6 fusion.2
  143.2 1.4 fusion.8
  146.7 4.7 %collective-permute-start.5 = (f32[256,128]{0,1:T(8,128)}, f32[256,128]{0,1:T(8,128)S(1)}, u32[]{:S(2)}, u32[]{:S(2)}) collective-permute-start(f32[256,128]{0,1:T(8,128)} %get-tuple-element.15), channel_id=1, source_target_pairs={{0,28},{4,0},{8,4},{12,8},{16,12},{20,16},{24,20},{28,24},{1,29},{... | collective-permute-start | bytes 393224 | tf_op jit(solution)/shard_map/ppermute | solution.py:10
  151.9 1.3 broadcast_select_fusion.8
  153.3 2.2 collective-permute-done.6
  158.3 1.0 copy.22
  163.4 2.0 collective-permute-start.9
  165.5 1.4 collective-permute-start.11
  167.8 1.3 gather_fusion.11
  169.2 1.0 copy.29
  170.2 1.2 broadcast_select_fusion.1
  171.4 1.0 copy.26
  172.4 1.4 gather_fusion.10
  173.8 1.0 copy.27
  174.8 1.3 broadcast_select_fusion.2
  176.1 1.0 copy.24
  177.1 1.3 gather_fusion.9
  178.5 1.0 copy.25
  180.1 1.0 copy.30
  181.1 1.3 gather_fusion.12
  182.5 1.0 copy.31
  183.5 1.5 fusion.15
  185.0 39.9 %all-reduce.1 = (f32[128]{0:T(128)S(1)}, f32[128]{0:T(128)S(1)}) all-reduce(f32[128]{0:T(128)S(1)} %broadcast_multiply_fusion.1, f32[128]{0:T(128)S(1)} %broadcast_multiply_fusion), channel_id=1, replica_groups=mesh['sub'=8,'col'=4] {'sub','col'}, use_global_device_ids=true, to_apply=%region_3.5 | all-reduce | flops 256 | bytes 2048 | tf_op jit(solution)/shard_map/psum | solution.py:45
  (116 shorter events, 23.7 us)
Async XLA Ops:
  0.0 140.9 %copy-start = (bf16[1,1024,1024]{2,1,0:T(8,128)(2,1)S(1)}, bf16[1,1024,1024]{2,1,0:T(8,128)(2,1)}, u32[]{:S(2)}) copy-start(bf16[1,1024,1024]{2,1,0:T(8,128)(2,1)} %param.11) | copy-start | bytes 6291460
  0.0 9.0 %copy-start.9 = (s32[1,1024]{1,0:T(1,128)S(1)}, s32[1,1024]{1,0:T(1,128)}, u32[]{:S(2)}) copy-start(s32[1,1024]{1,0:T(1,128)} %param.15) | copy-start | bytes 12292
  0.0 11.2 %copy-start.12 = (s32[1,8]{1,0:T(1,128)S(1)}, s32[1,8]{1,0:T(1,128)}, u32[]{:S(2)}) copy-start(s32[1,8]{1,0:T(1,128)} %param.14) | copy-start | bytes 100
  1.3 52.8 %collective-permute-start = (f32[256,128]{0,1:T(8,128)S(1)}, f32[256,128]{0,1:T(8,128)S(1)}, u32[]{:S(2)}, u32[]{:S(2)}) collective-permute-start(f32[256,128]{0,1:T(8,128)S(1)} %get-tuple-element.16), channel_id=1, source_target_pairs={{0,4},{4,8},{8,12},{12,16},{16,20},{20,24},{24,28},{28,0},{1,5},{5... | collective-permute-start | bytes 393224 | tf_op jit(solution)/shard_map/ppermute | solution.py:10
  4.4 50.7 %collective-permute-start.1 = (f32[256,128]{0,1:T(8,128)S(1)}, f32[256,128]{0,1:T(8,128)S(1)}, u32[]{:S(2)}, u32[]{:S(2)}) collective-permute-start(f32[256,128]{0,1:T(8,128)S(1)} %get-tuple-element.17), channel_id=1, source_target_pairs={{0,28},{4,0},{8,4},{12,8},{16,12},{20,16},{24,20},{28,24},{1,29},{... | collective-permute-start | bytes 393224 | tf_op jit(solution)/shard_map/ppermute | solution.py:10
  7.5 48.6 %collective-permute-start.3 = (f32[256,128]{0,1:T(8,128)S(1)}, f32[256,128]{0,1:T(8,128)S(1)}, u32[]{:S(2)}, u32[]{:S(2)}) collective-permute-start(f32[256,128]{0,1:T(8,128)S(1)} %get-tuple-element.18), channel_id=1, source_target_pairs={{0,3},{1,0},{2,1},{3,2},{4,7},{5,4},{6,5},{7,6},{8,11},{9,8},{10,9... | collective-permute-start | bytes 393224 | tf_op jit(solution)/shard_map/ppermute | solution.py:10
  9.0 42.5 %collective-permute-start.2 = (bf16[256,128]{1,0:T(8,128)(2,1)S(1)}, bf16[256,128]{1,0:T(8,128)(2,1)S(1)}, u32[]{:S(2)}, u32[]{:S(2)}) collective-permute-start(bf16[256,128]{1,0:T(8,128)(2,1)S(1)} %slice_bitcast_fusion.3), channel_id=1, source_target_pairs={{0,1},{1,2},{2,3},{3,0},{4,5},{5,6},{6,7},{7,4},{8,9},{9,10},{10,1... | collective-permute-start | bytes 196616 | tf_op jit(solution)/shard_map/ppermute | solution.py:10
  55.0 2.0 copy-start.6
  55.0 2.1 copy-start.8
  55.0 2.1 copy-start.4
  56.0 1.3 copy-start.2
  56.0 43.9 %copy-start.3 = (bf16[32,64]{1,0:T(8,128)(2,1)S(1)}, bf16[32,64]{1,0:T(8,128)(2,1)}, u32[]{:S(2)}) copy-start(bf16[32,64]{1,0:T(8,128)(2,1)} %param.13) | copy-start | bytes 12292
  57.1 86.1 %copy-start.10 = (pred[8]{0:T(512)(128)(4,1)S(1)}, pred[8]{0:T(512)(128)(4,1)}, u32[]{:S(2)}) copy-start(pred[8]{0:T(512)(128)(4,1)} %and_bitcast_fusion) | copy-start | bytes 28
  57.1 86.1 %copy-start.11 = (pred[8]{0:T(512)(128)(4,1)S(1)}, pred[8]{0:T(512)(128)(4,1)}, u32[]{:S(2)}) copy-start(pred[8]{0:T(512)(128)(4,1)} %compare_and_fusion.4) | copy-start | bytes 28
  146.7 9.7 %collective-permute-start.4 = (f32[256,128]{0,1:T(8,128)}, f32[256,128]{0,1:T(8,128)S(1)}, u32[]{:S(2)}, u32[]{:S(2)}) collective-permute-start(f32[256,128]{0,1:T(8,128)} %get-tuple-element.13), channel_id=1, source_target_pairs={{0,4},{4,8},{8,12},{12,16},{16,20},{20,24},{24,28},{28,0},{1,5},{5... | collective-permute-start | bytes 393224 | tf_op jit(solution)/shard_map/ppermute | solution.py:10
  146.7 10.6 %collective-permute-start.5 = (f32[256,128]{0,1:T(8,128)}, f32[256,128]{0,1:T(8,128)S(1)}, u32[]{:S(2)}, u32[]{:S(2)}) collective-permute-start(f32[256,128]{0,1:T(8,128)} %get-tuple-element.15), channel_id=1, source_target_pairs={{0,28},{4,0},{8,4},{12,8},{16,12},{20,16},{24,20},{28,24},{1,29},{... | collective-permute-start | bytes 393224 | tf_op jit(solution)/shard_map/ppermute | solution.py:10
  151.4 6.8 %collective-permute-start.7 = (f32[256,128]{0,1:T(8,128)}, f32[256,128]{0,1:T(8,128)}, u32[]{:S(2)}, u32[]{:S(2)}) collective-permute-start(f32[256,128]{0,1:T(8,128)} %get-tuple-element.14), channel_id=1, source_target_pairs={{0,3},{1,0},{2,1},{3,2},{4,7},{5,4},{6,5},{7,6},{8,11},{9,8},{10,9... | collective-permute-start | bytes 393224 | tf_op jit(solution)/shard_map/ppermute | solution.py:10
  151.4 4.0 %collective-permute-start.6 = (bf16[256,128]{0,1:T(8,128)(2,1)S(1)}, bf16[256,128]{0,1:T(8,128)(2,1)S(1)}, u32[]{:S(2)}, u32[]{:S(2)}) collective-permute-start(bf16[256,128]{0,1:T(8,128)(2,1)S(1)} %slice.134), channel_id=1, source_target_pairs={{0,1},{1,2},{2,3},{3,0},{4,5},{5,6},{6,7},{7,4},{8,9},{9,10},{10,1... | collective-permute-start | bytes 196616 | tf_op jit(solution)/shard_map/ppermute | solution.py:10
  160.1 1.6 copy-start.1
  162.6 4.3 %collective-permute-start.10 = (bf16[256,128]{0,1:T(8,128)(2,1)S(1)}, bf16[256,128]{0,1:T(8,128)(2,1)}, u32[]{:S(2)}, u32[]{:S(2)}) collective-permute-start(bf16[256,128]{0,1:T(8,128)(2,1)S(1)} %slice.133), channel_id=1, source_target_pairs={{0,1},{1,2},{2,3},{3,0},{4,5},{5,6},{6,7},{7,4},{8,9},{9,10},{10,1... | collective-permute-start | bytes 196616 | tf_op jit(solution)/shard_map/ppermute | solution.py:10
  163.4 8.0 %collective-permute-start.9 = (f32[256,128]{0,1:T(8,128)}, f32[256,128]{0,1:T(8,128)}, u32[]{:S(2)}, u32[]{:S(2)}) collective-permute-start(f32[256,128]{0,1:T(8,128)} %get-tuple-element.12), channel_id=1, source_target_pairs={{0,28},{4,0},{8,4},{12,8},{16,12},{20,16},{24,20},{28,24},{1,29},{... | collective-permute-start | bytes 393224 | tf_op jit(solution)/shard_map/ppermute | solution.py:10
  165.4 10.7 %collective-permute-start.8 = (f32[256,128]{0,1:T(8,128)}, f32[256,128]{0,1:T(8,128)}, u32[]{:S(2)}, u32[]{:S(2)}) collective-permute-start(f32[256,128]{0,1:T(8,128)} %get-tuple-element.10), channel_id=1, source_target_pairs={{0,4},{4,8},{8,12},{12,16},{16,20},{20,24},{24,28},{28,0},{1,5},{5... | collective-permute-start | bytes 393224 | tf_op jit(solution)/shard_map/ppermute | solution.py:10
  165.5 14.7 %collective-permute-start.11 = (f32[256,128]{0,1:T(8,128)}, f32[256,128]{0,1:T(8,128)}, u32[]{:S(2)}, u32[]{:S(2)}) collective-permute-start(f32[256,128]{0,1:T(8,128)} %get-tuple-element.11), channel_id=1, source_target_pairs={{0,3},{1,0},{2,1},{3,2},{4,7},{5,4},{6,5},{7,6},{8,11},{9,8},{10,9... | collective-permute-start | bytes 393224 | tf_op jit(solution)/shard_map/ppermute | solution.py:10
  169.2 10.3 %copy-start.7 = (pred[256]{0:T(512)(128)(4,1)S(1)}, pred[256]{0:T(512)(128)(4,1)}, u32[]{:S(2)}) copy-start(pred[256]{0:T(512)(128)(4,1)} %compare_and_fusion.3) | copy-start | bytes 772
  173.8 9.7 %copy-start.5 = (pred[256]{0:T(512)(128)(4,1)S(1)}, pred[256]{0:T(512)(128)(4,1)}, u32[]{:S(2)}) copy-start(pred[256]{0:T(512)(128)(4,1)} %compare_and_fusion) | copy-start | bytes 772
where the time goes:
time: 227 us; the launch traced here: 226 us
  blocking collectives  160 us (70%)
  local copies, waits for them, and re-layouts  28.1 us (12%)
  other arithmetic  15.7 us (7%)
  starting transfers between devices  15.5 us (7%)
  matrix products  4.13 us (2%)
    all_gather x1, blocking collectives, on_device(): values = lax.all_gather(coarse_load, ('sub', 'col'), axis=0, tiled=True)  41.2 us
    psum x1, blocking collectives, inner(): lax.psum(0.5 * jnp.sum(left_field * right_field, axis=0), ('sub', 'col'))  39.9 us
    unnamed x1, blocking collectives  37.7 us
    all_gather x1, blocking collectives, on_device(): piece = lax.all_gather(block_rows, 'sub', axis=0, tiled=True)  30.5 us
    gather x24, local copies, waits for them, and re-layouts, combine(): jnp.take(incoming[number].astype(jnp.float32), places[number], axis=0)  16 us
    ppermute x12, starting transfers between devices, from_behind(): return lax.ppermute(value, axis, pairs)  15.5 us
    psum x1, blocking collectives, on_device(): block_rows = lax.psum(partial_rows, 'col').astype(jnp.bfloat16)  10.3 us
    select_n x14, other arithmetic, combine(): jnp.take(incoming[number].astype(jnp.float32), places[number], axis=0)  8.71 us
  transfers between devices with their start and end apart: 12, of which 1 were waited for; matrix products, arithmetic and copies ran while one was open for 12% of the time, Pallas kernels for 0%

commit v1 on v0

--- a/solution.py
+++ b/solution.py
@@ -59,7 +59,15 @@
     partial_rows = jnp.dot(coarse_inverse, column_part, preferred_element_type=jnp.float32)
     start_taken = jnp.zeros((index_own.shape[0], cases), jnp.bfloat16)
     block_rows = lax.psum(partial_rows, "col").astype(jnp.bfloat16)
-    piece = lax.all_gather(block_rows, "sub", axis=0, tiled=True)
+    ways, here = (lax.axis_size("sub"), lax.axis_index("sub"))
+    grown, reach = (block_rows, 1)
+    while reach < ways:
+        theirs = lax.ppermute(grown, "sub", [(d, d ^ reach) for d in range(ways)])
+        mine_first = jnp.concatenate([grown, theirs], axis=0)
+        theirs_first = jnp.concatenate([theirs, grown], axis=0)
+        grown = jnp.where(here & reach == 0, mine_first, theirs_first)
+        reach = 2 * reach
+    piece = grown
     spots = index_own
     count = piece.shape[0]
     valid = (spots >= 0) & (spots < count)

time: 227 us -> 206 us (0.907)
  blocking collectives: 160 us -> 129 us
  waiting for transfers between devices: 2.19 us -> 11.8 us
    all_gather x1 -> x0, blocking collectives: 30.5 us -> none  [on_device(): piece = lax.all_gather(block_rows, 'sub', axis=0, tiled=True)]
    ppermute x0 -> x3, waiting for transfers between devices: none -> 9.21 us  [on_device(): theirs = lax.ppermute(grown, 'sub', [(d, d ^ reach) for d in range(ways)])]
  transfers between devices with their start and end apart: 12 -> 15, of which waited for: 1 -> 4; matrix products, arithmetic and copies ran while one was open for 12% -> 15% of each run, Pallas kernels for 0% -> 0%
where the time goes in v1:
time: 206 us; the launch traced here: 205 us
  blocking collectives  129 us (63%)
  local copies, waits for them, and re-layouts  28 us (14%)
  other arithmetic  15.7 us (8%)
  starting transfers between devices  15.5 us (8%)
  waiting for transfers between devices  11.8 us (6%)
  matrix products  4.13 us (2%)
    all_gather x1, blocking collectives, on_device(): values = lax.all_gather(coarse_load, ('sub', 'col'), axis=0, tiled=True)  41.2 us
    psum x1, blocking collectives, inner(): lax.psum(0.5 * jnp.sum(left_field * right_field, axis=0), ('sub', 'col'))  40.2 us
    unnamed x1, blocking collectives  37.7 us
    gather x24, local copies, waits for them, and re-layouts, combine(): jnp.take(incoming[number].astype(jnp.float32), places[number], axis=0)  16 us
    ppermute x12, starting transfers between devices, from_behind(): return lax.ppermute(value, axis, pairs)  15.3 us
    psum x1, blocking collectives, on_device(): block_rows = lax.psum(partial_rows, 'col').astype(jnp.bfloat16)  10.3 us
    ppermute x3, waiting for transfers between devices, on_device(): theirs = lax.ppermute(grown, 'sub', [(d, d ^ reach) for d in range(ways)])  9.21 us
    select_n x14, other arithmetic, combine(): jnp.take(incoming[number].astype(jnp.float32), places[number], axis=0)  8.71 us
  transfers between devices with their start and end apart: 15, of which 4 were waited for; matrix products, arithmetic and copies ran while one was open for 15% of the time, Pallas kernels for 0%

profile of v1, /device:TPU:0, one launch (start us, length us, event | category | flops | bytes accessed | tf_op | source)
XLA Modules:
  0.0 205.2 jit_solution(17697186114356030925)
XLA Ops:
  0.0 1.2 copy.8
  1.3 3.1 %collective-permute-start = (f32[256,128]{0,1:T(8,128)S(1)}, f32[256,128]{0,1:T(8,128)S(1)}, u32[]{:S(2)}, u32[]{:S(2)}) collective-permute-start(f32[256,128]{0,1:T(8,128)S(1)} %get-tuple-element.16), channel_id=1, source_target_pairs={{0,4},{4,8},{8,12},{12,16},{16,20},{20,24},{24,28},{28,0},{1,5},{5... | collective-permute-start | bytes 393224 | tf_op jit(solution)/shard_map/ppermute | solution.py:10
  4.4 3.1 %collective-permute-start.1 = (f32[256,128]{0,1:T(8,128)S(1)}, f32[256,128]{0,1:T(8,128)S(1)}, u32[]{:S(2)}, u32[]{:S(2)}) collective-permute-start(f32[256,128]{0,1:T(8,128)S(1)} %get-tuple-element.17), channel_id=1, source_target_pairs={{0,28},{4,0},{8,4},{12,8},{16,12},{20,16},{24,20},{28,24},{1,29},{... | collective-permute-start | bytes 393224 | tf_op jit(solution)/shard_map/ppermute | solution.py:10
  12.5 37.7 %all-reduce = s32[256]{0:T(256)S(1)} all-reduce(s32[256]{0:T(256)S(1)} %bitcast_dynamic-update-slice_fusion), channel_id=2, replica_groups=mesh['sub'=8,'col'=4] {'sub','col'}, use_global_device_ids=true, to_apply=%add | all-reduce | flops 256 | bytes 2048
  52.9 1.3 broadcast_select_fusion.9
  57.5 41.2 %all_gather.7 = bf16[256,128]{1,0:T(8,128)(2,1)S(1)} all-gather(bf16[8,128]{1,0:T(8,128)(2,1)S(1)} %fusion.9), channel_id=1, replica_groups=mesh['sub'=8,'col'=4] {'sub','col'}, dimensions={0}, use_global_device_ids=true | all-gather | bytes 67584 | tf_op jit(solution)/shard_map/all_gather | solution.py:54
  98.7 1.3 scatter_custom_fusion
  100.2 10.3 %psum.21 = bf16[32,128]{1,0:T(8,128)(2,1)S(1)} all-reduce(f32[32,128]{1,0:T(8,128)S(1)} %convolution_bitcast_fusion), channel_id=1, replica_groups=mesh['sub'=8,'col'=4] {'col'}, use_global_device_ids=true, to_apply=%region_1.3 | all-reduce | flops 4096 | bytes 24576 | tf_op jit(solution)/shard_map/psum | solution.py:61
  110.5 1.6 fusion.2
  112.1 2.0 collective-permute-done.4
  114.9 3.1 %collective-permute-done.5 = bf16[64,128]{1,0:T(8,128)(2,1)S(1)} collective-permute-done((bf16[64,128]{1,0:T(8,128)(2,1)S(1)}, bf16[64,128]{1,0:T(8,128)(2,1)S(1)}, u32[]{:S(2)}, u32[]{:S(2)}) %collective-permute-start.5) | collective-permute-done | bytes 16416 | tf_op jit(solution)/shard_map/ppermute | solution.py:65
  118.7 4.1 %collective-permute-done.6 = bf16[128,128]{1,0:T(8,128)(2,1)S(1)} collective-permute-done((bf16[128,128]{1,0:T(8,128)(2,1)S(1)}, bf16[128,128]{1,0:T(8,128)(2,1)S(1)}, u32[]{:S(2)}, u32[]{:S(2)}) %collective-permute-start.6) | collective-permute-done | bytes 32800 | tf_op jit(solution)/shard_map/ppermute | solution.py:65
  123.6 1.4 fusion.8
  125.8 4.7 %collective-permute-start.8 = (f32[256,128]{0,1:T(8,128)}, f32[256,128]{0,1:T(8,128)S(1)}, u32[]{:S(2)}, u32[]{:S(2)}) collective-permute-start(f32[256,128]{0,1:T(8,128)} %get-tuple-element.15), channel_id=1, source_target_pairs={{0,28},{4,0},{8,4},{12,8},{16,12},{20,16},{24,20},{28,24},{1,29},{... | collective-permute-start | bytes 393224 | tf_op jit(solution)/shard_map/ppermute | solution.py:10
  131.0 1.2 broadcast_select_fusion.8
  132.2 2.6 %collective-permute-done.9 = bf16[256,128]{0,1:T(8,128)(2,1)S(1)} collective-permute-done((bf16[256,128]{0,1:T(8,128)(2,1)S(1)}, bf16[256,128]{0,1:T(8,128)(2,1)S(1)}, u32[]{:S(2)}, u32[]{:S(2)}) %collective-permute-start.9) | collective-permute-done | bytes 65568 | tf_op jit(solution)/shard_map/ppermute | solution.py:10
  137.7 1.0 copy.22
  142.8 1.6 collective-permute-start.12
  144.8 1.2 collective-permute-start.14
  147.0 1.3 gather_fusion.11
  148.3 1.0 copy.29
  149.3 1.3 broadcast_select_fusion.1
  150.6 1.0 copy.26
  151.6 1.3 gather_fusion.10
  152.9 1.0 copy.27
  153.9 1.3 broadcast_select_fusion.2
  156.2 1.3 gather_fusion.9
  157.6 1.0 copy.25
  160.3 1.3 gather_fusion.12
  161.6 1.0 copy.31
  162.6 1.5 fusion.15
  164.1 40.2 %all-reduce.1 = (f32[128]{0:T(128)S(1)}, f32[128]{0:T(128)S(1)}) all-reduce(f32[128]{0:T(128)S(1)} %broadcast_multiply_fusion.1, f32[128]{0:T(128)S(1)} %broadcast_multiply_fusion), channel_id=1, replica_groups=mesh['sub'=8,'col'=4] {'sub','col'}, use_global_device_ids=true, to_apply=%region_3.5 | all-reduce | flops 256 | bytes 2048 | tf_op jit(solution)/shard_map/psum | solution.py:45
  (124 shorter events, 26.2 us)
Async XLA Ops:
  0.0 110.5 %copy-start = (bf16[1,1024,1024]{2,1,0:T(8,128)(2,1)S(1)}, bf16[1,1024,1024]{2,1,0:T(8,128)(2,1)}, u32[]{:S(2)}) copy-start(bf16[1,1024,1024]{2,1,0:T(8,128)(2,1)} %param.11) | copy-start | bytes 6291460
  0.0 9.0 %copy-start.9 = (s32[1,1024]{1,0:T(1,128)S(1)}, s32[1,1024]{1,0:T(1,128)}, u32[]{:S(2)}) copy-start(s32[1,1024]{1,0:T(1,128)} %param.15) | copy-start | bytes 12292
  0.0 11.2 %copy-start.12 = (s32[1,8]{1,0:T(1,128)S(1)}, s32[1,8]{1,0:T(1,128)}, u32[]{:S(2)}) copy-start(s32[1,8]{1,0:T(1,128)} %param.14) | copy-start | bytes 100
  1.3 52.9 %collective-permute-start = (f32[256,128]{0,1:T(8,128)S(1)}, f32[256,128]{0,1:T(8,128)S(1)}, u32[]{:S(2)}, u32[]{:S(2)}) collective-permute-start(f32[256,128]{0,1:T(8,128)S(1)} %get-tuple-element.16), channel_id=1, source_target_pairs={{0,4},{4,8},{8,12},{12,16},{16,20},{20,24},{24,28},{28,0},{1,5},{5... | collective-permute-start | bytes 393224 | tf_op jit(solution)/shard_map/ppermute | solution.py:10
  4.4 50.8 %collective-permute-start.1 = (f32[256,128]{0,1:T(8,128)S(1)}, f32[256,128]{0,1:T(8,128)S(1)}, u32[]{:S(2)}, u32[]{:S(2)}) collective-permute-start(f32[256,128]{0,1:T(8,128)S(1)} %get-tuple-element.17), channel_id=1, source_target_pairs={{0,28},{4,0},{8,4},{12,8},{16,12},{20,16},{24,20},{28,24},{1,29},{... | collective-permute-start | bytes 393224 | tf_op jit(solution)/shard_map/ppermute | solution.py:10
  7.5 48.7 %collective-permute-start.3 = (f32[256,128]{0,1:T(8,128)S(1)}, f32[256,128]{0,1:T(8,128)S(1)}, u32[]{:S(2)}, u32[]{:S(2)}) collective-permute-start(f32[256,128]{0,1:T(8,128)S(1)} %get-tuple-element.18), channel_id=1, source_target_pairs={{0,3},{1,0},{2,1},{3,2},{4,7},{5,4},{6,5},{7,6},{8,11},{9,8},{10,9... | collective-permute-start | bytes 393224 | tf_op jit(solution)/shard_map/ppermute | solution.py:10
  9.0 42.4 %collective-permute-start.2 = (bf16[256,128]{1,0:T(8,128)(2,1)S(1)}, bf16[256,128]{1,0:T(8,128)(2,1)S(1)}, u32[]{:S(2)}, u32[]{:S(2)}) collective-permute-start(bf16[256,128]{1,0:T(8,128)(2,1)S(1)} %slice_bitcast_fusion.3), channel_id=1, source_target_pairs={{0,1},{1,2},{2,3},{3,0},{4,5},{5,6},{6,7},{7,4},{8,9},{9,10},{10,1... | collective-permute-start | bytes 196616 | tf_op jit(solution)/shard_map/ppermute | solution.py:10
  55.1 2.0 copy-start.6
  55.1 2.1 %copy-start.8 = (pred[256]{0:T(512)(128)(4,1)S(1)}, pred[256]{0:T(512)(128)(4,1)}, u32[]{:S(2)}) copy-start(pred[256]{0:T(512)(128)(4,1)} %compare_and_fusion.2) | copy-start | bytes 772
  55.1 2.1 %copy-start.4 = (pred[256]{0:T(512)(128)(4,1)S(1)}, pred[256]{0:T(512)(128)(4,1)}, u32[]{:S(2)}) copy-start(pred[256]{0:T(512)(128)(4,1)} %compare_and_fusion) | copy-start | bytes 772
  56.1 1.2 copy-start.2
  56.1 43.9 %copy-start.3 = (bf16[32,64]{1,0:T(8,128)(2,1)S(1)}, bf16[32,64]{1,0:T(8,128)(2,1)}, u32[]{:S(2)}) copy-start(bf16[32,64]{1,0:T(8,128)(2,1)} %param.13) | copy-start | bytes 12292
  57.3 66.2 %copy-start.10 = (pred[8]{0:T(512)(128)(4,1)S(1)}, pred[8]{0:T(512)(128)(4,1)}, u32[]{:S(2)}) copy-start(pred[8]{0:T(512)(128)(4,1)} %and_bitcast_fusion) | copy-start | bytes 28
  57.3 66.2 %copy-start.11 = (pred[8]{0:T(512)(128)(4,1)S(1)}, pred[8]{0:T(512)(128)(4,1)}, u32[]{:S(2)}) copy-start(pred[8]{0:T(512)(128)(4,1)} %compare_and_fusion.4) | copy-start | bytes 28
  110.5 3.7 %collective-permute-start.4 = (bf16[32,128]{1,0:T(8,128)(2,1)S(1)}, bf16[32,128]{1,0:T(8,128)(2,1)S(1)}, u32[]{:S(2)}, u32[]{:S(2)}) collective-permute-start(bf16[32,128]{1,0:T(8,128)(2,1)S(1)} %psum.21), channel_id=1, source_target_pairs={{0,4},{4,0},{8,12},{12,8},{16,20},{20,16},{24,28},{28,24},{1,5},{5... | collective-permute-start | bytes 24584 | tf_op jit(solution)/shard_map/ppermute | solution.py:65
  114.2 3.8 %collective-permute-start.5 = (bf16[64,128]{1,0:T(8,128)(2,1)S(1)}, bf16[64,128]{1,0:T(8,128)(2,1)S(1)}, u32[]{:S(2)}, u32[]{:S(2)}) collective-permute-start(bf16[64,128]{1,0:T(8,128)(2,1)S(1)} %maximum_select_fusion.2), channel_id=1, source_target_pairs={{0,8},{4,12},{8,0},{12,4},{16,24},{20,28},{24,16},{28,20},{1,9},{5... | collective-permute-start | bytes 49160 | tf_op jit(solution)/shard_map/ppermute | solution.py:65
  118.0 4.9 %collective-permute-start.6 = (bf16[128,128]{1,0:T(8,128)(2,1)S(1)}, bf16[128,128]{1,0:T(8,128)(2,1)S(1)}, u32[]{:S(2)}, u32[]{:S(2)}) collective-permute-start(bf16[128,128]{1,0:T(8,128)(2,1)S(1)} %maximum_select_fusion.1), channel_id=1, source_target_pairs={{0,16},{4,20},{8,24},{12,28},{16,0},{20,4},{24,8},{28,12},{1,17},{... | collective-permute-start | bytes 98312 | tf_op jit(solution)/shard_map/ppermute | solution.py:65
  125.7 10.1 %collective-permute-start.7 = (f32[256,128]{0,1:T(8,128)}, f32[256,128]{0,1:T(8,128)S(1)}, u32[]{:S(2)}, u32[]{:S(2)}) collective-permute-start(f32[256,128]{0,1:T(8,128)} %get-tuple-element.13), channel_id=1, source_target_pairs={{0,4},{4,8},{8,12},{12,16},{16,20},{20,24},{24,28},{28,0},{1,5},{5... | collective-permute-start | bytes 393224 | tf_op jit(solution)/shard_map/ppermute | solution.py:10
  125.8 10.9 %collective-permute-start.8 = (f32[256,128]{0,1:T(8,128)}, f32[256,128]{0,1:T(8,128)S(1)}, u32[]{:S(2)}, u32[]{:S(2)}) collective-permute-start(f32[256,128]{0,1:T(8,128)} %get-tuple-element.15), channel_id=1, source_target_pairs={{0,28},{4,0},{8,4},{12,8},{16,12},{20,16},{24,20},{28,24},{1,29},{... | collective-permute-start | bytes 393224 | tf_op jit(solution)/shard_map/ppermute | solution.py:10
  130.5 7.2 %collective-permute-start.10 = (f32[256,128]{0,1:T(8,128)}, f32[256,128]{0,1:T(8,128)}, u32[]{:S(2)}, u32[]{:S(2)}) collective-permute-start(f32[256,128]{0,1:T(8,128)} %get-tuple-element.14), channel_id=1, source_target_pairs={{0,3},{1,0},{2,1},{3,2},{4,7},{5,4},{6,5},{7,6},{8,11},{9,8},{10,9... | collective-permute-start | bytes 393224 | tf_op jit(solution)/shard_map/ppermute | solution.py:10
  130.5 4.3 %collective-permute-start.9 = (bf16[256,128]{0,1:T(8,128)(2,1)S(1)}, bf16[256,128]{0,1:T(8,128)(2,1)S(1)}, u32[]{:S(2)}, u32[]{:S(2)}) collective-permute-start(bf16[256,128]{0,1:T(8,128)(2,1)S(1)} %slice.134), channel_id=1, source_target_pairs={{0,1},{1,2},{2,3},{3,0},{4,5},{5,6},{6,7},{7,4},{8,9},{9,10},{10,1... | collective-permute-start | bytes 196616 | tf_op jit(solution)/shard_map/ppermute | solution.py:10
  139.5 1.6 copy-start.1
  142.0 4.0 %collective-permute-start.13 = (bf16[256,128]{0,1:T(8,128)(2,1)S(1)}, bf16[256,128]{0,1:T(8,128)(2,1)}, u32[]{:S(2)}, u32[]{:S(2)}) collective-permute-start(bf16[256,128]{0,1:T(8,128)(2,1)S(1)} %slice.133), channel_id=1, source_target_pairs={{0,1},{1,2},{2,3},{3,0},{4,5},{5,6},{6,7},{7,4},{8,9},{9,10},{10,1... | collective-permute-start | bytes 196616 | tf_op jit(solution)/shard_map/ppermute | solution.py:10
  142.8 7.8 %collective-permute-start.12 = (f32[256,128]{0,1:T(8,128)}, f32[256,128]{0,1:T(8,128)}, u32[]{:S(2)}, u32[]{:S(2)}) collective-permute-start(f32[256,128]{0,1:T(8,128)} %get-tuple-element.12), channel_id=1, source_target_pairs={{0,28},{4,0},{8,4},{12,8},{16,12},{20,16},{24,20},{28,24},{1,29},{... | collective-permute-start | bytes 393224 | tf_op jit(solution)/shard_map/ppermute | solution.py:10
  144.5 10.8 %collective-permute-start.11 = (f32[256,128]{0,1:T(8,128)}, f32[256,128]{0,1:T(8,128)}, u32[]{:S(2)}, u32[]{:S(2)}) collective-permute-start(f32[256,128]{0,1:T(8,128)} %get-tuple-element.10), channel_id=1, source_target_pairs={{0,4},{4,8},{8,12},{12,16},{16,20},{20,24},{24,28},{28,0},{1,5},{5... | collective-permute-start | bytes 393224 | tf_op jit(solution)/shard_map/ppermute | solution.py:10
  144.8 14.4 %collective-permute-start.14 = (f32[256,128]{0,1:T(8,128)}, f32[256,128]{0,1:T(8,128)}, u32[]{:S(2)}, u32[]{:S(2)}) collective-permute-start(f32[256,128]{0,1:T(8,128)} %get-tuple-element.11), channel_id=1, source_target_pairs={{0,3},{1,0},{2,1},{3,2},{4,7},{5,4},{6,5},{7,6},{8,11},{9,8},{10,9... | collective-permute-start | bytes 393224 | tf_op jit(solution)/shard_map/ppermute | solution.py:10
  148.3 10.3 %copy-start.7 = (pred[256]{0:T(512)(128)(4,1)S(1)}, pred[256]{0:T(512)(128)(4,1)}, u32[]{:S(2)}) copy-start(pred[256]{0:T(512)(128)(4,1)} %compare_and_fusion.3) | copy-start | bytes 772
  152.9 9.7 %copy-start.5 = (pred[256]{0:T(512)(128)(4,1)S(1)}, pred[256]{0:T(512)(128)(4,1)}, u32[]{:S(2)}) copy-start(pred[256]{0:T(512)(128)(4,1)} %compare_and_fusion) | copy-start | bytes 772
